TPU v7x, 256 devices: a whole 4x4x8 slice. The times are simulated.
256 devices in a mesh: ctx: 32 (over z_hi, y, x), tp: 8 (over z_lo, core).
Axes of the slice: x: 4, y: 4, z: 8 (z_hi: 2, z_lo: 4; z = z_hi * 4 + z_lo), core: 2. Of those that a mesh axis runs over, the one named last changes fastest.
Arguments:
- query_rows: bfloat16 [8192, 8192], P(('ctx', 'tp')), may hold values from -2 to 2
- key_rows: bfloat16 [8192, 1024], P(('ctx', 'tp')), may hold values from -2 to 2
- value_rows: bfloat16 [8192, 1024], P(('ctx', 'tp')), may hold values from -6 to 6
- doc_ids: int32 [64], replicated, may hold values from 0 to 15, never falling along the last dimension, each value on 1 to 14 neighbouring positions
- grad_out: bfloat16 [8192, 8192], P(('ctx', 'tp')), may hold values from -6 to 6
Outputs:
- attention: bfloat16 [8192, 8192], P(('ctx', 'tp'))
- grad_queries: float32 [8192, 8192], P(('ctx', 'tp'))
- grad_keys: float32 [8192, 1024], P(('ctx', 'tp'))
- grad_values: float32 [8192, 1024], P(('ctx', 'tp'))
Inputs may be any that keep to these rules, and one draw needn't show every extreme that they name: `doc_ids`: block document ids never fall; each document covers 1 to 14 whole blocks, and some document exactly 14.
All inputs are finite; a program needn't handle non-finite values.
Results may differ from a plain program's by a relative error of at most 0.0048.
Values may be sent and summed in bfloat16 or wider, within the bound.
A program may use at most 128 MiB of HBM per device.

v0:
```python
import functools
import jax
import jax.numpy as jnp
from jax import lax
from jax.experimental import pallas as pl
from jax.experimental.pallas import tpu as pltpu
from jax.sharding import PartitionSpec as P

HEAD_DIM = 128
BLOCK = 128
NX = 4
MESH = pl.DeviceIdType.MESH
LOG2E = 1.4426950408889634
NEG = -1e30
F32 = jnp.float32
BF16 = jnp.bfloat16
NT = (((1,), (1,)), ((), ()))
NN = (((1,), (0,)), ((), ()))


def dot(a, b, dims=NN):
    return lax.dot_general(a, b, dims, preferred_element_type=F32)


def kernel(rows_n, tp_n, group, tok, docs, q_in, k_in, v_in, g_in,
           attn_out, dq_out, dk_out, dv_out,
           qh, gh, kvs, cbuf, kt, vt, bias, wts, inv_t, odot,
           attn_b, dqt, dq_b, dacc, dsend, r_m, r_b, y_b, y_c, ry1, ry2, own_b,
           land_a, land_q, land_k,
           kv_s, kv_r, q_s, q_r, g_s, g_r, loc,
           xm_s, xm_r, xb_s, xb_r, y_s, y_r,
           dm_s, dm_r, db_s, db_r, dy_s, dy_r,
           oa_s, oa_r, oq_s, oq_r, ok_s, ok_r):
    stretch = rows_n_tokens = kvs.shape[2]
    scale = HEAD_DIM ** -0.5
    gw = group * HEAD_DIM
    c = lax.axis_index("ctx")
    p = lax.axis_index("tp")
    row = c // NX
    x = lax.rem(c, NX)

    def tp_at(i):
        return lax.rem(p + i, tp_n)

    def mate_x(i):
        return lax.rem(x + i, NX)

    def ctx_at(r, xx):
        return r * NX + xx

    def rcopy(src, dst, ss, rs, dev):
        return pltpu.make_async_remote_copy(
            src_ref=src, dst_ref=dst, send_sem=ss, recv_sem=rs, device_id=dev, device_id_type=MESH)

    barrier = pltpu.get_barrier_semaphore()
    for i in range(1, tp_n):
        pl.semaphore_signal(barrier, inc=1, device_id={"ctx": c, "tp": tp_at(i)}, device_id_type=MESH)
    for i in range(1, NX):
        pl.semaphore_signal(barrier, inc=1, device_id={"ctx": ctx_at(row, mate_x(i)), "tp": p}, device_id_type=MESH)
    for k in (1, 2, rows_n - 1, rows_n - 2):
        pl.semaphore_signal(
            barrier, inc=1, device_id={"ctx": ctx_at(lax.rem(row + k, rows_n), x), "tp": p}, device_id_type=MESH)
    pl.semaphore_wait(barrier, tp_n - 1 + NX - 1 + 4)

    my_rows = pl.ds(pl.multiple_of(p * tok, tok), tok)

    def cols(t, w):
        return pl.ds(pl.multiple_of(t * w, w), w)

    kv_copies = []
    for i in range(1, tp_n):
        t = tp_at(i)
        for n, src in ((0, k_in), (1, v_in)):
            cp = rcopy(src.at[:, cols(t, HEAD_DIM)], kvs.at[x, n, my_rows, :], kv_s.at[n, i - 1], kv_r.at[n, i - 1],
                       {"ctx": c, "tp": t})
            cp.start()
            kv_copies.append(cp)
    locals_ = [
        pltpu.make_async_copy(k_in.at[:, cols(p, HEAD_DIM)], kvs.at[x, 0, my_rows, :], loc.at[0]),
        pltpu.make_async_copy(v_in.at[:, cols(p, HEAD_DIM)], kvs.at[x, 1, my_rows, :], loc.at[1]),
        pltpu.make_async_copy(q_in.at[:, cols(p, gw)], qh.at[my_rows, :], loc.at[2]),
        pltpu.make_async_copy(g_in.at[:, cols(p, gw)], gh.at[my_rows, :], loc.at[3]),
    ]
    for cp in locals_:
        cp.start()
    q_copies = []
    for i in range(1, tp_n):
        t = tp_at(i)
        cp = rcopy(q_in.at[:, cols(t, gw)], qh.at[my_rows, :], q_s.at[i - 1], q_r.at[i - 1], {"ctx": c, "tp": t})
        cp.start()
        q_copies.append(cp)

    @pl.when(row < 2)
    def _():
        for i in range(1, NX):
            @pl.when(mate_x(i) > x)
            def _():
                kvs[mate_x(i)] = jnp.zeros(kvs.shape[1:], BF16)

    @pl.when(row < 1)
    def _():
        kvs[NX:] = jnp.zeros((NX,) + kvs.shape[1:], BF16)

    lane = lax.broadcasted_iota(jnp.int32, (1, stretch), 1)
    per = stretch // BLOCK
    q_doc = [docs[c * per + b] for b in range(per)]
    for slot in range(2 * NX):
        xs = slot % NX
        if slot < NX:
            src = jnp.where(xs <= x, c - x + xs, c - x + xs - 2 * NX)
        else:
            src = c - x + xs - NX
        own = (src == c).astype(jnp.int32)
        for b in range(per):
            k_doc = jnp.where(src >= 0, docs[jnp.maximum(src, 0) * per + b], -1)
            line = jnp.where(lane < BLOCK, jnp.where(k_doc == q_doc[0], 0.0, NEG), jnp.where(k_doc == q_doc[1], 0.0, NEG))
            key_at = lax.broadcasted_iota(jnp.int32, (BLOCK, stretch), 0) + b * BLOCK
            q_at = lax.broadcasted_iota(jnp.int32, (BLOCK, stretch), 1)
            late = (key_at - q_at) * own > 0
            bias[slot, b * BLOCK:(b + 1) * BLOCK, :] = jnp.where(late, NEG, jnp.broadcast_to(line, (BLOCK, stretch)))

    locals_[0].wait()
    locals_[1].wait()
    for cp in kv_copies:
        cp.wait_recv()

    def x_own(i):
        return rcopy(kvs.at[x], kvs.at[x], xm_s.at[i - 1], xm_r.at[i - 1], {"ctx": ctx_at(row, mate_x(i)), "tp": p})

    def x_far(i):
        return rcopy(cbuf, kvs.at[x], xm_s.at[i - 1], xm_r.at[i - 1], {"ctx": ctx_at(row, mate_x(i)), "tp": p})

    def x_prev(i):
        return rcopy(kvs.at[NX + x], kvs.at[NX + x], xb_s.at[i - 1], xb_r.at[i - 1],
                     {"ctx": ctx_at(row, mate_x(i)), "tp": p})

    to_next = rcopy(kvs.at[x], kvs.at[NX + x], y_s.at[0], y_r.at[0], {"ctx": c + NX, "tp": p})
    to_second = rcopy(kvs.at[x], cbuf, y_s.at[1], y_r.at[1], {"ctx": c + 2 * NX, "tp": p})
    has_next = row + 1 < rows_n
    has_second = (row + 2 < rows_n) & (x > 0)
    from_prev = row >= 1
    from_second = (row >= 2) & (x > 0)

    @pl.when(has_next)
    def _():
        to_next.start()

    @pl.when(has_second)
    def _():
        to_second.start()

    for i in range(1, NX):
        @pl.when(mate_x(i) > x)
        def _():
            x_own(i).start()

    g_copies = []
    for i in range(1, tp_n):
        t = tp_at(i)
        cp = rcopy(g_in.at[:, cols(t, gw)], gh.at[my_rows, :], g_s.at[i - 1], g_r.at[i - 1], {"ctx": c, "tp": t})
        cp.start()
        g_copies.append(cp)

    @pl.when(from_prev)
    def _():
        to_next.wait_recv()
        for i in range(1, NX):
            x_prev(i).start()

    @pl.when(from_second)
    def _():
        to_second.wait_recv()
        for i in range(1, NX):
            @pl.when(mate_x(i) < x)
            def _():
                x_far(i).start()

    for i in range(1, NX):
        @pl.when((lax.rem(x + NX - i, NX) < x) | (row >= 2))
        def _():
            x_own(i).wait_recv()

    @pl.when(from_prev)
    def _():
        for i in range(1, NX):
            x_prev(i).wait_recv()

    for slot in range(2 * NX):
        kt[:, slot * stretch:(slot + 1) * stretch] = jnp.transpose(kvs[slot, 0].astype(F32)).astype(BF16)
        vt[:, slot * stretch:(slot + 1) * stretch] = jnp.transpose(kvs[slot, 1].astype(F32)).astype(BF16)

    locals_[2].wait()
    for cp in q_copies:
        cp.wait_recv()

    def forward(h, carry):
        at = pl.ds(pl.multiple_of(h * HEAD_DIM, HEAD_DIM), HEAD_DIM)
        q = qh[:, at]
        total = jnp.zeros((1, stretch), F32)
        out_t = jnp.zeros((HEAD_DIM, stretch), F32)
        for slot in range(2 * NX):
            s = dot(kvs[slot, 0], q, NT)
            w = jnp.exp2(s * (scale * LOG2E) + bias[slot])
            wts[h, slot] = w
            total = total + jnp.sum(w, axis=0, keepdims=True)
            out_t = out_t + dot(vt[:, slot * stretch:(slot + 1) * stretch], w.astype(BF16))
        inv_t[h] = 1.0 / total
        attn_b[:, at] = jnp.transpose(out_t / total).astype(BF16)
        return carry

    lax.fori_loop(0, group, forward, 0)

    a_copies = []
    for i in range(1, tp_n):
        t = tp_at(i)
        cp = rcopy(attn_b.at[cols(t, tok), :], land_a.at[:, cols(p, gw)], oa_s.at[i - 1], oa_r.at[i - 1],
                   {"ctx": c, "tp": t})
        cp.start()
        a_copies.append(cp)

    locals_[3].wait()
    for cp in g_copies:
        cp.wait_recv()

    def dots(h, carry):
        at = pl.ds(pl.multiple_of(h * HEAD_DIM, HEAD_DIM), HEAD_DIM)
        prod = gh[:, at].astype(F32) * attn_b[:, at].astype(F32)
        odot[h] = jnp.sum(jnp.transpose(prod), axis=0, keepdims=True)
        dqt[h] = jnp.zeros((HEAD_DIM, stretch), F32)
        return carry

    lax.fori_loop(0, group, dots, 0)

    def d_m(i):
        return rcopy(dsend.at[mate_x(i)], r_m.at[i - 1], dm_s.at[i - 1], dm_r.at[i - 1],
                     {"ctx": ctx_at(row, mate_x(i)), "tp": p})

    def d_b(i):
        return rcopy(dsend.at[NX + mate_x(i)], r_b.at[i - 1], db_s.at[i - 1], db_r.at[i - 1],
                     {"ctx": ctx_at(row, mate_x(i)), "tp": p})

    def backward(slot):
        dacc[...] = jnp.zeros_like(dacc)
        k_t = kt[:, pl.ds(pl.multiple_of(slot * stretch, stretch), stretch)]

        def head(h, carry):
            at = pl.ds(pl.multiple_of(h * HEAD_DIM, HEAD_DIM), HEAD_DIM)
            q = qh[:, at]
            g = gh[:, at]
            pr = wts[h, slot] * inv_t[h]
            dp = dot(kvs[slot, 1], g, NT)
            ds = (pr * (dp - odot[h])).astype(BF16)
            dacc[1] += dot(pr.astype(BF16), g)
            dacc[0] += dot(ds, q)
            dqt[h] += dot(k_t, ds)
            return carry

        lax.fori_loop(0, group, head, 0)

    for i in (1, 2, 3, 0):
        slot = NX + mate_x(i)
        backward(slot)
        dsend[slot, 0] = (dacc[0] * scale).astype(BF16)
        dsend[slot, 1] = dacc[1].astype(BF16)
        if i:
            d_b(i).start()
    for i in (1, 2, 3, 0):
        slot = mate_x(i)
        backward(slot)
        if i:
            dsend[slot, 0] = (dacc[0] * scale).astype(BF16)
            dsend[slot, 1] = dacc[1].astype(BF16)
            d_m(i).start()

    for h in range(group):
        dq_b[:, h * HEAD_DIM:(h + 1) * HEAD_DIM] = (jnp.transpose(dqt[h]) * scale).astype(BF16)
    dq_copies = []
    for i in range(1, tp_n):
        t = tp_at(i)
        cp = rcopy(dq_b.at[cols(t, tok), :], land_q.at[:, cols(p, gw)], oq_s.at[i - 1], oq_r.at[i - 1],
                   {"ctx": c, "tp": t})
        cp.start()
        dq_copies.append(cp)

    for i in range(1, NX):
        d_b(i).wait_recv()
    y_b[...] = (dsend[NX + x].astype(F32) + r_b[0].astype(F32) + r_b[1].astype(F32) + r_b[2].astype(F32)).astype(BF16)
    back_one = rcopy(y_b, ry1, dy_s.at[0], dy_r.at[0], {"ctx": c - NX, "tp": p})
    back_two = rcopy(y_c, ry2, dy_s.at[1], dy_r.at[1], {"ctx": c - 2 * NX, "tp": p})

    @pl.when(from_prev)
    def _():
        back_one.start()

    for i in range(1, NX):
        d_m(i).wait_recv()
    dacc[0] = dacc[0] * scale
    far = jnp.zeros(dacc.shape, F32)
    near = dacc[...]
    for i in range(1, NX):
        xs = lax.rem(x + NX - i, NX)
        got = r_m[i - 1].astype(F32)
        far = far + jnp.where(xs < x, got, 0.0)
        near = near + jnp.where(xs > x, got, 0.0)
    y_c[...] = far.astype(BF16)
    dacc[...] = near

    @pl.when(from_second)
    def _():
        back_two.start()

    @pl.when(has_next)
    def _():
        back_one.wait_recv()
        dacc[...] += ry1[...].astype(F32)

    @pl.when(has_second)
    def _():
        back_two.wait_recv()
        dacc[...] += ry2[...].astype(F32)

    own_b[...] = dacc[...].astype(BF16)
    k_copies = []
    for i in range(1, tp_n):
        t = tp_at(i)
        cp = rcopy(own_b.at[:, cols(t, tok), :], land_k.at[:, :, cols(p, HEAD_DIM)], ok_s.at[i - 1], ok_r.at[i - 1],
                   {"ctx": c, "tp": t})
        cp.start()
        k_copies.append(cp)

    land_a[:, cols(p, gw)] = attn_b[my_rows, :]
    land_q[:, cols(p, gw)] = dq_b[my_rows, :]
    land_k[:, :, cols(p, HEAD_DIM)] = own_b[:, my_rows, :]
    for cp in a_copies:
        cp.wait_recv()
    attn_out[...] = land_a[...]
    for cp in dq_copies:
        cp.wait_recv()
    dq_out[...] = land_q[...].astype(F32)
    for cp in k_copies:
        cp.wait_recv()
    dk_out[...] = land_k[0].astype(F32)
    dv_out[...] = land_k[1].astype(F32)

    for cp in kv_copies + q_copies + g_copies + a_copies + dq_copies + k_copies:
        cp.wait_send()
    for i in range(1, NX):
        @pl.when((mate_x(i) > x) | (row >= 2))
        def _():
            x_own(i).wait_send()
        d_m(i).wait_send()
        d_b(i).wait_send()

    @pl.when(from_prev)
    def _():
        for i in range(1, NX):
            x_prev(i).wait_send()
        back_one.wait_send()

    @pl.when(from_second)
    def _():
        back_two.wait_send()

    @pl.when(has_next)
    def _():
        to_next.wait_send()

    @pl.when(has_second)
    def _():
        to_second.wait_send()


def solution(mesh):
    ctx_n, tp_n = mesh.shape["ctx"], mesh.shape["tp"]
    rows_n = ctx_n // NX

    def local(query_rows, key_rows, value_rows, doc_ids, grad_out):
        tok, width = query_rows.shape
        kw = key_rows.shape[1]
        stretch = tok * tp_n
        gw = width // tp_n
        group = gw // HEAD_DIM
        n2 = 2 * NX
        dma = pltpu.SemaphoreType.DMA
        piece = (2, stretch, HEAD_DIM)
        V = pltpu.VMEM
        anyspec = pl.BlockSpec(memory_space=pl.ANY)
        vspec = pl.BlockSpec(memory_space=pltpu.VMEM)
        scratch = [
            V((stretch, gw), BF16), V((stretch, gw), BF16), V((n2,) + piece, BF16), V(piece, BF16),
            V((HEAD_DIM, n2 * stretch), BF16), V((HEAD_DIM, n2 * stretch), BF16), V((n2, stretch, stretch), F32),
            V((group, n2, stretch, stretch), F32), V((group, 1, stretch), F32), V((group, 1, stretch), F32),
            V((stretch, gw), BF16), V((group, HEAD_DIM, stretch), F32), V((stretch, gw), BF16),
            V(piece, F32), V((n2,) + piece, BF16), V((NX - 1,) + piece, BF16), V((NX - 1,) + piece, BF16),
            V(piece, BF16), V(piece, BF16), V(piece, BF16), V(piece, BF16), V(piece, BF16),
            V((tok, width), BF16), V((tok, width), BF16), V((2, tok, kw), BF16),
            dma((2, tp_n - 1)), dma((2, tp_n - 1)), dma((tp_n - 1,)), dma((tp_n - 1,)), dma((tp_n - 1,)),
            dma((tp_n - 1,)), dma((4,)),
            dma((NX - 1,)), dma((NX - 1,)), dma((NX - 1,)), dma((NX - 1,)), dma((2,)), dma((2,)),
            dma((NX - 1,)), dma((NX - 1,)), dma((NX - 1,)), dma((NX - 1,)), dma((2,)), dma((2,)),
            dma((tp_n - 1,)), dma((tp_n - 1,)), dma((tp_n - 1,)), dma((tp_n - 1,)), dma((tp_n - 1,)), dma((tp_n - 1,)),
        ]
        return pl.pallas_call(
            functools.partial(kernel, rows_n, tp_n, group, tok),
            out_shape=(
                jax.ShapeDtypeStruct((tok, width), BF16),
                jax.ShapeDtypeStruct((tok, width), F32),
                jax.ShapeDtypeStruct((tok, kw), F32),
                jax.ShapeDtypeStruct((tok, kw), F32),
            ),
            in_specs=[pl.BlockSpec(memory_space=pltpu.SMEM)] + [anyspec] * 4,
            out_specs=(vspec,) * 4,
            scratch_shapes=scratch,
            compiler_params=pltpu.CompilerParams(
                collective_id=0, has_side_effects=True, vmem_limit_bytes=60 * 1024 * 1024),
            name="attention_layer",
        )(doc_ids, query_rows, key_rows, value_rows, grad_out)

    rows = P(("ctx", "tp"), None)
    return jax.shard_map(
        local, mesh=mesh, in_specs=(rows, rows, rows, P(), rows), out_specs=(rows,) * 4, check_vma=False)
```

profile of v0, /device:TPU:19, one launch (start us, length us, event | category | flops | bytes accessed | tf_op | source)
XLA Modules:
  0.0 111.3 jit_solution(2604869086298657738)
XLA Ops:
  0.6 106.1 %attention_layer.1 = (bf16[32,8192]{1,0:T(8,128)(2,1)}, f32[32,8192]{1,0:T(8,128)}, f32[32,1024]{1,0:T(8,128)}, f32[32,1024]{1,0:T(8,128)}) custom-call(s32[64]{0:T(128)} %docs.1, bf16[32,8192]{1,0:T(8,128)(2,1)} %q_in.1, bf16[32,1024]{1,0:T(8,128)(2,1)} %k_in.1, bf16[32,1024]{1,0:T(8,128)(2,1)} %v_in.1, bf16[32,8192]{1,0:T(8,128)(2,1)} %g_in.1), custom_call_target="tpu_custom_call" | custom-call | tf_op jit(solution)/shard_map/attention_layer/pallas_call | solution.py:403
  106.7 0.0 copy-start
  106.7 2.0 %copy.13 = bf16[32,8192]{1,0:T(8,128)(2,1)} copy(bf16[32,8192]{1,0:T(8,128)(2,1)} %get-tuple-element.8) | data formatting | bytes 1048576
  108.7 0.0 copy-done
  108.7 0.0 copy-start.2
  108.7 1.0 copy.14
  109.7 0.1 copy-done.2
  109.7 0.0 copy-start.1
  109.7 0.7 copy.15
  110.4 0.3 copy-done.1
  110.7 0.7 copy.16
Async XLA Ops:
  106.7 2.0 %copy-start = (f32[32,8192]{1,0:T(8,128)S(1)}, f32[32,8192]{1,0:T(8,128)}, u32[]{:S(2)}) copy-start(f32[32,8192]{1,0:T(8,128)} %get-tuple-element.9) | copy-start | bytes 3145732
  108.7 1.0 copy-start.2
  109.7 1.0 copy-start.1
where the time goes:
time: 112 us; the launch traced here: 111 us
  Pallas kernels  106 us (95%)
  local copies, waits for them, and re-layouts  4.59 us (4%)
    pallas_call x1, Pallas kernels, local(): pl.pallas_call(functools.partial(kernel, rows_n, tp_n, group, tok), out_s...  106 us
    unnamed x10, local copies, waits for them, and re-layouts  4.59 us

commit v1 on v0

--- a/solution.py
+++ b/solution.py
@@ -42,11 +42,22 @@
     def tp_at(i):
         return lax.rem(p + i, tp_n)
 
+    def flip(r, t):
+        return t + lax.rem(r // (rows_n // 2), 2) * (tp_n - 2 - 4 * (t // 2))
+
+    def head_at(t):
+        return flip(row, t)
+
+    me = head_at(p)
+
     def mate_x(i):
         return lax.rem(x + i, NX)
 
     def ctx_at(r, xx):
         return r * NX + xx
+
+    def row_at(k):
+        return {"ctx": c + k * NX, "tp": flip(row + k, me)}
 
     def rcopy(src, dst, ss, rs, dev):
         return pltpu.make_async_remote_copy(
@@ -58,8 +69,9 @@
     for i in range(1, NX):
         pl.semaphore_signal(barrier, inc=1, device_id={"ctx": ctx_at(row, mate_x(i)), "tp": p}, device_id_type=MESH)
     for k in (1, 2, rows_n - 1, rows_n - 2):
+        r = lax.rem(row + k, rows_n)
         pl.semaphore_signal(
-            barrier, inc=1, device_id={"ctx": ctx_at(lax.rem(row + k, rows_n), x), "tp": p}, device_id_type=MESH)
+            barrier, inc=1, device_id={"ctx": ctx_at(r, x), "tp": flip(r, me)}, device_id_type=MESH)
     pl.semaphore_wait(barrier, tp_n - 1 + NX - 1 + 4)
 
     my_rows = pl.ds(pl.multiple_of(p * tok, tok), tok)
@@ -71,22 +83,22 @@
     for i in range(1, tp_n):
         t = tp_at(i)
         for n, src in ((0, k_in), (1, v_in)):
-            cp = rcopy(src.at[:, cols(t, HEAD_DIM)], kvs.at[x, n, my_rows, :], kv_s.at[n, i - 1], kv_r.at[n, i - 1],
+            cp = rcopy(src.at[:, cols(head_at(t), HEAD_DIM)], kvs.at[x, n, my_rows, :], kv_s.at[n, i - 1], kv_r.at[n, i - 1],
                        {"ctx": c, "tp": t})
             cp.start()
             kv_copies.append(cp)
     locals_ = [
-        pltpu.make_async_copy(k_in.at[:, cols(p, HEAD_DIM)], kvs.at[x, 0, my_rows, :], loc.at[0]),
-        pltpu.make_async_copy(v_in.at[:, cols(p, HEAD_DIM)], kvs.at[x, 1, my_rows, :], loc.at[1]),
-        pltpu.make_async_copy(q_in.at[:, cols(p, gw)], qh.at[my_rows, :], loc.at[2]),
-        pltpu.make_async_copy(g_in.at[:, cols(p, gw)], gh.at[my_rows, :], loc.at[3]),
+        pltpu.make_async_copy(k_in.at[:, cols(me, HEAD_DIM)], kvs.at[x, 0, my_rows, :], loc.at[0]),
+        pltpu.make_async_copy(v_in.at[:, cols(me, HEAD_DIM)], kvs.at[x, 1, my_rows, :], loc.at[1]),
+        pltpu.make_async_copy(q_in.at[:, cols(me, gw)], qh.at[my_rows, :], loc.at[2]),
+        pltpu.make_async_copy(g_in.at[:, cols(me, gw)], gh.at[my_rows, :], loc.at[3]),
     ]
     for cp in locals_:
         cp.start()
     q_copies = []
     for i in range(1, tp_n):
         t = tp_at(i)
-        cp = rcopy(q_in.at[:, cols(t, gw)], qh.at[my_rows, :], q_s.at[i - 1], q_r.at[i - 1], {"ctx": c, "tp": t})
+        cp = rcopy(q_in.at[:, cols(head_at(t), gw)], qh.at[my_rows, :], q_s.at[i - 1], q_r.at[i - 1], {"ctx": c, "tp": t})
         cp.start()
         q_copies.append(cp)
 
@@ -134,8 +146,8 @@
         return rcopy(kvs.at[NX + x], kvs.at[NX + x], xb_s.at[i - 1], xb_r.at[i - 1],
                      {"ctx": ctx_at(row, mate_x(i)), "tp": p})
 
-    to_next = rcopy(kvs.at[x], kvs.at[NX + x], y_s.at[0], y_r.at[0], {"ctx": c + NX, "tp": p})
-    to_second = rcopy(kvs.at[x], cbuf, y_s.at[1], y_r.at[1], {"ctx": c + 2 * NX, "tp": p})
+    to_next = rcopy(kvs.at[x], kvs.at[NX + x], y_s.at[0], y_r.at[0], row_at(1))
+    to_second = rcopy(kvs.at[x], cbuf, y_s.at[1], y_r.at[1], row_at(2))
     has_next = row + 1 < rows_n
     has_second = (row + 2 < rows_n) & (x > 0)
     from_prev = row >= 1
@@ -157,7 +169,7 @@
     g_copies = []
     for i in range(1, tp_n):
         t = tp_at(i)
-        cp = rcopy(g_in.at[:, cols(t, gw)], gh.at[my_rows, :], g_s.at[i - 1], g_r.at[i - 1], {"ctx": c, "tp": t})
+        cp = rcopy(g_in.at[:, cols(head_at(t), gw)], gh.at[my_rows, :], g_s.at[i - 1], g_r.at[i - 1], {"ctx": c, "tp": t})
         cp.start()
         g_copies.append(cp)
 
@@ -213,7 +225,7 @@
     a_copies = []
     for i in range(1, tp_n):
         t = tp_at(i)
-        cp = rcopy(attn_b.at[cols(t, tok), :], land_a.at[:, cols(p, gw)], oa_s.at[i - 1], oa_r.at[i - 1],
+        cp = rcopy(attn_b.at[cols(t, tok), :], land_a.at[:, cols(me, gw)], oa_s.at[i - 1], oa_r.at[i - 1],
                    {"ctx": c, "tp": t})
         cp.start()
         a_copies.append(cp)
@@ -277,7 +289,7 @@
     dq_copies = []
     for i in range(1, tp_n):
         t = tp_at(i)
-        cp = rcopy(dq_b.at[cols(t, tok), :], land_q.at[:, cols(p, gw)], oq_s.at[i - 1], oq_r.at[i - 1],
+        cp = rcopy(dq_b.at[cols(t, tok), :], land_q.at[:, cols(me, gw)], oq_s.at[i - 1], oq_r.at[i - 1],
                    {"ctx": c, "tp": t})
         cp.start()
         dq_copies.append(cp)
@@ -285,8 +297,8 @@
     for i in range(1, NX):
         d_b(i).wait_recv()
     y_b[...] = (dsend[NX + x].astype(F32) + r_b[0].astype(F32) + r_b[1].astype(F32) + r_b[2].astype(F32)).astype(BF16)
-    back_one = rcopy(y_b, ry1, dy_s.at[0], dy_r.at[0], {"ctx": c - NX, "tp": p})
-    back_two = rcopy(y_c, ry2, dy_s.at[1], dy_r.at[1], {"ctx": c - 2 * NX, "tp": p})
+    back_one = rcopy(y_b, ry1, dy_s.at[0], dy_r.at[0], row_at(-1))
+    back_two = rcopy(y_c, ry2, dy_s.at[1], dy_r.at[1], row_at(-2))
 
     @pl.when(from_prev)
     def _():
@@ -323,14 +335,14 @@
     k_copies = []
     for i in range(1, tp_n):
         t = tp_at(i)
-        cp = rcopy(own_b.at[:, cols(t, tok), :], land_k.at[:, :, cols(p, HEAD_DIM)], ok_s.at[i - 1], ok_r.at[i - 1],
+        cp = rcopy(own_b.at[:, cols(t, tok), :], land_k.at[:, :, cols(me, HEAD_DIM)], ok_s.at[i - 1], ok_r.at[i - 1],
                    {"ctx": c, "tp": t})
         cp.start()
         k_copies.append(cp)
 
-    land_a[:, cols(p, gw)] = attn_b[my_rows, :]
-    land_q[:, cols(p, gw)] = dq_b[my_rows, :]
-    land_k[:, :, cols(p, HEAD_DIM)] = own_b[:, my_rows, :]
+    land_a[:, cols(me, gw)] = attn_b[my_rows, :]
+    land_q[:, cols(me, gw)] = dq_b[my_rows, :]
+    land_k[:, :, cols(me, HEAD_DIM)] = own_b[:, my_rows, :]
     for cp in a_copies:
         cp.wait_recv()
     attn_out[...] = land_a[...]

time: 112 us -> 104 us (0.929)
  Pallas kernels: 106 us -> 98.5 us
    pallas_call x1, Pallas kernels: 106 us -> 98.5 us  [local(): pl.pallas_call(functools.partial(kernel, rows_n, tp_n, group, tok), out_s...]
where the time goes in v1:
time: 104 us
  Pallas kernels  98.5 us (95%)
  local copies, waits for them, and re-layouts  4.59 us (4%)
    pallas_call x1, Pallas kernels, local(): pl.pallas_call(functools.partial(kernel, rows_n, tp_n, group, tok), out_s...  98.5 us
    unnamed x10, local copies, waits for them, and re-layouts  4.59 us

profile of v1, /device:TPU:19, one launch (start us, length us, event | category | flops | bytes accessed | tf_op | source)
XLA Modules:
  0.0 103.7 jit_solution(16409202669813078171)
XLA Ops:
  0.6 98.5 %attention_layer.1 = (bf16[32,8192]{1,0:T(8,128)(2,1)}, f32[32,8192]{1,0:T(8,128)}, f32[32,1024]{1,0:T(8,128)}, f32[32,1024]{1,0:T(8,128)}) custom-call(s32[64]{0:T(128)} %docs.1, bf16[32,8192]{1,0:T(8,128)(2,1)} %q_in.1, bf16[32,1024]{1,0:T(8,128)(2,1)} %k_in.1, bf16[32,1024]{1,0:T(8,128)(2,1)} %v_in.1, bf16[32,8192]{1,0:T(8,128)(2,1)} %g_in.1), custom_call_target="tpu_custom_call" | custom-call | tf_op jit(solution)/shard_map/attention_layer/pallas_call | solution.py:415
  99.1 0.0 copy-start
  99.1 2.0 %copy.13 = bf16[32,8192]{1,0:T(8,128)(2,1)} copy(bf16[32,8192]{1,0:T(8,128)(2,1)} %get-tuple-element.8) | data formatting | bytes 1048576
  101.1 0.0 copy-done
  101.1 0.0 copy-start.2
  101.1 1.0 copy.14
  102.1 0.1 copy-done.2
  102.1 0.0 copy-start.1
  102.1 0.7 copy.15
  102.8 0.3 copy-done.1
  103.1 0.7 copy.16
Async XLA Ops:
  99.1 2.0 %copy-start = (f32[32,8192]{1,0:T(8,128)S(1)}, f32[32,8192]{1,0:T(8,128)}, u32[]{:S(2)}) copy-start(f32[32,8192]{1,0:T(8,128)} %get-tuple-element.9) | copy-start | bytes 3145732
  101.1 1.0 copy-start.2
  102.1 1.0 copy-start.1

commit v2 on v1

--- a/solution.py
+++ b/solution.py
@@ -23,15 +23,14 @@
 
 
 def kernel(rows_n, tp_n, group, tok, docs, q_in, k_in, v_in, g_in,
-           attn_out, dq_out, dk_out, dv_out,
+           attn_out, dq_out, dkv_out,
            qh, gh, kvs, cbuf, kt, vt, bias, wts, inv_t, odot,
-           attn_b, dqt, dq_b, dacc, dsend, r_m, r_b, y_b, y_c, ry1, ry2, own_b,
-           land_a, land_q, land_k,
+           attn_b, dqt, dq_b, dacc, near, dsend, r_m, r_b, y_b, y_c, ry1, ry2, own_b,
            kv_s, kv_r, q_s, q_r, g_s, g_r, loc,
            xm_s, xm_r, xb_s, xb_r, y_s, y_r,
            dm_s, dm_r, db_s, db_r, dy_s, dy_r,
            oa_s, oa_r, oq_s, oq_r, ok_s, ok_r):
-    stretch = rows_n_tokens = kvs.shape[2]
+    stretch = kvs.shape[2]
     scale = HEAD_DIM ** -0.5
     gw = group * HEAD_DIM
     c = lax.axis_index("ctx")
@@ -99,8 +98,15 @@
     for i in range(1, tp_n):
         t = tp_at(i)
         cp = rcopy(q_in.at[:, cols(head_at(t), gw)], qh.at[my_rows, :], q_s.at[i - 1], q_r.at[i - 1], {"ctx": c, "tp": t})
-        cp.start()
         q_copies.append(cp)
+    mid = rows_n // 2
+    out_z = (row == mid - 1) | (row == mid - 2)
+    back_z = (row == mid) | (row == mid + 1)
+
+    @pl.when(jnp.logical_not(out_z))
+    def _():
+        for cp in q_copies:
+            cp.start()
 
     @pl.when(row < 2)
     def _():
@@ -166,6 +172,11 @@
         def _():
             x_own(i).start()
 
+    @pl.when(out_z)
+    def _():
+        for cp in q_copies:
+            cp.start()
+
     g_copies = []
     for i in range(1, tp_n):
         t = tp_at(i)
@@ -225,10 +236,12 @@
     a_copies = []
     for i in range(1, tp_n):
         t = tp_at(i)
-        cp = rcopy(attn_b.at[cols(t, tok), :], land_a.at[:, cols(me, gw)], oa_s.at[i - 1], oa_r.at[i - 1],
+        cp = rcopy(attn_b.at[cols(t, tok), :], attn_out.at[:, cols(me, gw)], oa_s.at[i - 1], oa_r.at[i - 1],
                    {"ctx": c, "tp": t})
         cp.start()
         a_copies.append(cp)
+    keep_a = pltpu.make_async_copy(attn_b.at[my_rows, :], attn_out.at[:, cols(me, gw)], loc.at[0])
+    keep_a.start()
 
     locals_[3].wait()
     for cp in g_copies:
@@ -238,7 +251,6 @@
         at = pl.ds(pl.multiple_of(h * HEAD_DIM, HEAD_DIM), HEAD_DIM)
         prod = gh[:, at].astype(F32) * attn_b[:, at].astype(F32)
         odot[h] = jnp.sum(jnp.transpose(prod), axis=0, keepdims=True)
-        dqt[h] = jnp.zeros((HEAD_DIM, stretch), F32)
         return carry
 
     lax.fori_loop(0, group, dots, 0)
@@ -251,108 +263,144 @@
         return rcopy(dsend.at[NX + mate_x(i)], r_b.at[i - 1], db_s.at[i - 1], db_r.at[i - 1],
                      {"ctx": ctx_at(row, mate_x(i)), "tp": p})
 
+    half = group // 2
+    hw = half * HEAD_DIM
+
+    def grads(h, slot, q, g, k_t):
+        pr = wts[h, slot] * inv_t[h]
+        dp = dot(kvs[slot, 1], g, NT)
+        ds = (pr * (dp - odot[h])).astype(BF16)
+        return dot(ds, q), dot(pr.astype(BF16), g), dot(k_t, ds)
+
+    def put_dq(h, total):
+        at = pl.ds(pl.multiple_of(h * HEAD_DIM, HEAD_DIM), HEAD_DIM)
+        dq_b[:, at] = (jnp.transpose(total) * scale).astype(BF16)
+
+    dacc[...] = jnp.zeros_like(dacc)
+
+    def first(h, carry):
+        at = pl.ds(pl.multiple_of(h * HEAD_DIM, HEAD_DIM), HEAD_DIM)
+        q = qh[:, at]
+        g = gh[:, at]
+        total = jnp.zeros((HEAD_DIM, stretch), F32)
+        for slot in range(2 * NX):
+            dk, dv, dq = grads(h, slot, q, g, kt[:, slot * stretch:(slot + 1) * stretch])
+            dacc[slot, 0] += dk
+            dacc[slot, 1] += dv
+            total = total + dq
+        put_dq(h, total)
+        dqt[h] = jnp.zeros((HEAD_DIM, stretch), F32)
+        return carry
+
+    lax.fori_loop(0, half, first, 0)
+
+    dq_copies = []
+    for n in range(2):
+        for i in range(1, tp_n):
+            t = tp_at(i)
+            to = pl.ds(pl.multiple_of(me * gw + n * hw, HEAD_DIM), hw)
+            dq_copies.append(rcopy(
+                dq_b.at[cols(t, tok), n * hw:(n + 1) * hw], dq_out.at[:, to], oq_s.at[n, i - 1], oq_r.at[n, i - 1],
+                {"ctx": c, "tp": t}))
+    for cp in dq_copies[:tp_n - 1]:
+        cp.start()
+
     def backward(slot):
-        dacc[...] = jnp.zeros_like(dacc)
         k_t = kt[:, pl.ds(pl.multiple_of(slot * stretch, stretch), stretch)]
 
-        def head(h, carry):
+        def head(j, carry):
+            h = half + j
             at = pl.ds(pl.multiple_of(h * HEAD_DIM, HEAD_DIM), HEAD_DIM)
-            q = qh[:, at]
-            g = gh[:, at]
-            pr = wts[h, slot] * inv_t[h]
-            dp = dot(kvs[slot, 1], g, NT)
-            ds = (pr * (dp - odot[h])).astype(BF16)
-            dacc[1] += dot(pr.astype(BF16), g)
-            dacc[0] += dot(ds, q)
-            dqt[h] += dot(k_t, ds)
+            dk, dv, dq = grads(h, slot, qh[:, at], gh[:, at], k_t)
+            dacc[slot, 0] += dk
+            dacc[slot, 1] += dv
+            dqt[j] += dq
             return carry
 
-        lax.fori_loop(0, group, head, 0)
-
-    for i in (1, 2, 3, 0):
-        slot = NX + mate_x(i)
+        lax.fori_loop(0, half, head, 0, unroll=True)
+
+    def ready(slot):
         backward(slot)
-        dsend[slot, 0] = (dacc[0] * scale).astype(BF16)
-        dsend[slot, 1] = dacc[1].astype(BF16)
-        if i:
-            d_b(i).start()
-    for i in (1, 2, 3, 0):
-        slot = mate_x(i)
-        backward(slot)
-        if i:
-            dsend[slot, 0] = (dacc[0] * scale).astype(BF16)
-            dsend[slot, 1] = dacc[1].astype(BF16)
-            d_m(i).start()
-
-    for h in range(group):
-        dq_b[:, h * HEAD_DIM:(h + 1) * HEAD_DIM] = (jnp.transpose(dqt[h]) * scale).astype(BF16)
-    dq_copies = []
-    for i in range(1, tp_n):
-        t = tp_at(i)
-        cp = rcopy(dq_b.at[cols(t, tok), :], land_q.at[:, cols(me, gw)], oq_s.at[i - 1], oq_r.at[i - 1],
-                   {"ctx": c, "tp": t})
-        cp.start()
-        dq_copies.append(cp)
-
-    for i in range(1, NX):
-        d_b(i).wait_recv()
-    y_b[...] = (dsend[NX + x].astype(F32) + r_b[0].astype(F32) + r_b[1].astype(F32) + r_b[2].astype(F32)).astype(BF16)
+        dsend[slot, 0] = (dacc[slot, 0] * scale).astype(BF16)
+        dsend[slot, 1] = dacc[slot, 1].astype(BF16)
+
+    for i in range(1, NX):
+        ready(mate_x(i))
+        d_m(i).start()
+    for i in range(1, NX):
+        ready(NX + mate_x(i))
+        d_b(i).start()
+
     back_one = rcopy(y_b, ry1, dy_s.at[0], dy_r.at[0], row_at(-1))
     back_two = rcopy(y_c, ry2, dy_s.at[1], dy_r.at[1], row_at(-2))
-
-    @pl.when(from_prev)
-    def _():
-        back_one.start()
-
+    backward(x)
     for i in range(1, NX):
         d_m(i).wait_recv()
-    dacc[0] = dacc[0] * scale
-    far = jnp.zeros(dacc.shape, F32)
-    near = dacc[...]
+    far = jnp.zeros(near.shape, F32)
+    near[0] = dacc[x, 0] * scale
+    near[1] = dacc[x, 1]
     for i in range(1, NX):
         xs = lax.rem(x + NX - i, NX)
         got = r_m[i - 1].astype(F32)
         far = far + jnp.where(xs < x, got, 0.0)
-        near = near + jnp.where(xs > x, got, 0.0)
+        near[...] += jnp.where(xs > x, got, 0.0)
     y_c[...] = far.astype(BF16)
-    dacc[...] = near
 
     @pl.when(from_second)
     def _():
         back_two.start()
 
+    ready(NX + x)
+
+    for j in range(half):
+        put_dq(half + j, dqt[j])
+
+    @pl.when(jnp.logical_not(back_z))
+    def _():
+        for cp in dq_copies[tp_n - 1:]:
+            cp.start()
+
+    for i in range(1, NX):
+        d_b(i).wait_recv()
+    y_b[...] = (dsend[NX + x].astype(F32) + r_b[0].astype(F32) + r_b[1].astype(F32) + r_b[2].astype(F32)).astype(BF16)
+
+    @pl.when(from_prev)
+    def _():
+        back_one.start()
+
+    @pl.when(back_z)
+    def _():
+        for cp in dq_copies[tp_n - 1:]:
+            cp.start()
+
+    keep_q = pltpu.make_async_copy(dq_b.at[my_rows, :], dq_out.at[:, cols(me, gw)], loc.at[1])
+    keep_q.start()
+
+    @pl.when(has_second)
+    def _():
+        back_two.wait_recv()
+        near[...] += ry2[...].astype(F32)
+
     @pl.when(has_next)
     def _():
         back_one.wait_recv()
-        dacc[...] += ry1[...].astype(F32)
-
-    @pl.when(has_second)
-    def _():
-        back_two.wait_recv()
-        dacc[...] += ry2[...].astype(F32)
-
-    own_b[...] = dacc[...].astype(BF16)
+        near[...] += ry1[...].astype(F32)
+
+    own_b[...] = near[...].astype(BF16)
     k_copies = []
     for i in range(1, tp_n):
         t = tp_at(i)
-        cp = rcopy(own_b.at[:, cols(t, tok), :], land_k.at[:, :, cols(me, HEAD_DIM)], ok_s.at[i - 1], ok_r.at[i - 1],
+        cp = rcopy(own_b.at[:, cols(t, tok), :], dkv_out.at[:, :, cols(me, HEAD_DIM)], ok_s.at[i - 1], ok_r.at[i - 1],
                    {"ctx": c, "tp": t})
         cp.start()
         k_copies.append(cp)
-
-    land_a[:, cols(me, gw)] = attn_b[my_rows, :]
-    land_q[:, cols(me, gw)] = dq_b[my_rows, :]
-    land_k[:, :, cols(me, HEAD_DIM)] = own_b[:, my_rows, :]
-    for cp in a_copies:
+    keep_k = pltpu.make_async_copy(own_b.at[:, my_rows, :], dkv_out.at[:, :, cols(me, HEAD_DIM)], loc.at[2])
+    keep_k.start()
+
+    for cp in a_copies + dq_copies + k_copies:
         cp.wait_recv()
-    attn_out[...] = land_a[...]
-    for cp in dq_copies:
-        cp.wait_recv()
-    dq_out[...] = land_q[...].astype(F32)
-    for cp in k_copies:
-        cp.wait_recv()
-    dk_out[...] = land_k[0].astype(F32)
-    dv_out[...] = land_k[1].astype(F32)
+    for cp in (keep_a, keep_q, keep_k):
+        cp.wait()
 
     for cp in kv_copies + q_copies + g_copies + a_copies + dq_copies + k_copies:
         cp.wait_send()
@@ -397,36 +445,34 @@
         piece = (2, stretch, HEAD_DIM)
         V = pltpu.VMEM
         anyspec = pl.BlockSpec(memory_space=pl.ANY)
-        vspec = pl.BlockSpec(memory_space=pltpu.VMEM)
         scratch = [
             V((stretch, gw), BF16), V((stretch, gw), BF16), V((n2,) + piece, BF16), V(piece, BF16),
             V((HEAD_DIM, n2 * stretch), BF16), V((HEAD_DIM, n2 * stretch), BF16), V((n2, stretch, stretch), F32),
             V((group, n2, stretch, stretch), F32), V((group, 1, stretch), F32), V((group, 1, stretch), F32),
-            V((stretch, gw), BF16), V((group, HEAD_DIM, stretch), F32), V((stretch, gw), BF16),
-            V(piece, F32), V((n2,) + piece, BF16), V((NX - 1,) + piece, BF16), V((NX - 1,) + piece, BF16),
+            V((stretch, gw), BF16), V((group // 2, HEAD_DIM, stretch), F32), V((stretch, gw), BF16),
+            V((n2,) + piece, F32), V(piece, F32), V((n2,) + piece, BF16), V((NX - 1,) + piece, BF16), V((NX - 1,) + piece, BF16),
             V(piece, BF16), V(piece, BF16), V(piece, BF16), V(piece, BF16), V(piece, BF16),
-            V((tok, width), BF16), V((tok, width), BF16), V((2, tok, kw), BF16),
             dma((2, tp_n - 1)), dma((2, tp_n - 1)), dma((tp_n - 1,)), dma((tp_n - 1,)), dma((tp_n - 1,)),
             dma((tp_n - 1,)), dma((4,)),
             dma((NX - 1,)), dma((NX - 1,)), dma((NX - 1,)), dma((NX - 1,)), dma((2,)), dma((2,)),
             dma((NX - 1,)), dma((NX - 1,)), dma((NX - 1,)), dma((NX - 1,)), dma((2,)), dma((2,)),
-            dma((tp_n - 1,)), dma((tp_n - 1,)), dma((tp_n - 1,)), dma((tp_n - 1,)), dma((tp_n - 1,)), dma((tp_n - 1,)),
+            dma((tp_n - 1,)), dma((tp_n - 1,)), dma((2, tp_n - 1)), dma((2, tp_n - 1)), dma((tp_n - 1,)), dma((tp_n - 1,)),
         ]
-        return pl.pallas_call(
+        attn, dq, dkv = pl.pallas_call(
             functools.partial(kernel, rows_n, tp_n, group, tok),
             out_shape=(
                 jax.ShapeDtypeStruct((tok, width), BF16),
-                jax.ShapeDtypeStruct((tok, width), F32),
-                jax.ShapeDtypeStruct((tok, kw), F32),
-                jax.ShapeDtypeStruct((tok, kw), F32),
+                jax.ShapeDtypeStruct((tok, width), BF16),
+                jax.ShapeDtypeStruct((2, tok, kw), BF16),
             ),
             in_specs=[pl.BlockSpec(memory_space=pltpu.SMEM)] + [anyspec] * 4,
-            out_specs=(vspec,) * 4,
+            out_specs=(anyspec,) * 3,
             scratch_shapes=scratch,
             compiler_params=pltpu.CompilerParams(
                 collective_id=0, has_side_effects=True, vmem_limit_bytes=60 * 1024 * 1024),
             name="attention_layer",
         )(doc_ids, query_rows, key_rows, value_rows, grad_out)
+        return attn, dq.astype(F32), dkv[0].astype(F32), dkv[1].astype(F32)
 
     rows = P(("ctx", "tp"), None)
     return jax.shard_map(

time: 104 us -> 86.8 us (0.83)
  the two profiles are of different devices: /device:TPU:19 before, /device:TPU:31 now
where the time goes in v2:
time: 86.8 us; the launch traced here: 86.7 us
  Pallas kernels  82.4 us (95%)
  other arithmetic  2.86 us (3%)
    pallas_call x1, Pallas kernels, local(): pl.pallas_call(functools.partial(kernel, rows_n, tp_n, group, tok), out_s...  82.4 us
    convert_element_type x2, other arithmetic, local(): return (attn, dq.astype(F32), dkv[0].astype(F32), dkv[1].astype(F32))  2.86 us

profile of v2, /device:TPU:31, one launch (start us, length us, event | category | flops | bytes accessed | tf_op | source)
XLA Modules:
  0.0 86.7 jit_solution(16305227982963024144)
XLA Ops:
  0.6 82.4 %attention_layer.1 = (bf16[32,8192]{1,0:T(8,128)(2,1)}, bf16[32,8192]{1,0:T(8,128)(2,1)}, bf16[2,32,1024]{2,1,0:T(8,128)(2,1)}) custom-call(s32[64]{0:T(128)} %docs.1, bf16[32,8192]{1,0:T(8,128)(2,1)} %q_in.1, bf16[32,1024]{1,0:T(8,128)(2,1)} %k_in.1, bf16[32,1024]{1,0:T(8,128)(2,1)} %v_in.1, bf16[32,8192]{1,0:T(8,128)(2,1)} %g_in.1), custom_call_target="tpu_custom_call" | custom-call | tf_op jit(solution)/shard_map/attention_layer/pallas_call | solution.py:461
  83.0 0.0 copy-start.1
  83.0 0.0 copy-start
  83.0 2.1 %convert_element_type.15 = f32[32,8192]{1,0:T(8,128)} convert(bf16[32,8192]{1,0:T(8,128)(2,1)} %get-tuple-element.8) | non-fusion elementwise | flops 262144 | bytes 1572864 | tf_op jit(solution)/shard_map/convert_element_type | solution.py:475
  85.2 0.0 copy-done.1
  85.2 0.7 bitcast_convert_fusion
  85.9 0.0 copy-done
  85.9 0.8 copy.10
Async XLA Ops:
  83.0 2.2 %copy-start.1 = (bf16[2,32,1024]{2,1,0:T(8,128)(2,1)S(1)}, bf16[2,32,1024]{2,1,0:T(8,128)(2,1)}, u32[]{:S(2)}) copy-start(bf16[2,32,1024]{2,1,0:T(8,128)(2,1)} %get-tuple-element.9) | copy-start | bytes 393220
  83.0 2.9 %copy-start = (bf16[32,8192]{1,0:T(8,128)(2,1)S(1)}, bf16[32,8192]{1,0:T(8,128)(2,1)}, u32[]{:S(2)}) copy-start(bf16[32,8192]{1,0:T(8,128)(2,1)} %get-tuple-element.16) | copy-start | bytes 1572868

commit v3 on v2

--- a/solution.py
+++ b/solution.py
@@ -152,6 +152,11 @@
         return rcopy(kvs.at[NX + x], kvs.at[NX + x], xb_s.at[i - 1], xb_r.at[i - 1],
                      {"ctx": ctx_at(row, mate_x(i)), "tp": p})
 
+    left, right = mate_x(NX - 1), mate_x(1)
+    pass_k = rcopy(kvs.at[NX + left, 0], kvs.at[NX + left, 0], xb_s.at[1], xb_r.at[1],
+                   {"ctx": ctx_at(row, right), "tp": p})
+    pass_v = rcopy(kvs.at[NX + right, 1], kvs.at[NX + right, 1], xb_s.at[3], xb_r.at[3],
+                   {"ctx": ctx_at(row, left), "tp": p})
     to_next = rcopy(kvs.at[x], kvs.at[NX + x], y_s.at[0], y_r.at[0], row_at(1))
     to_second = rcopy(kvs.at[x], cbuf, y_s.at[1], y_r.at[1], row_at(2))
     has_next = row + 1 < rows_n
@@ -177,18 +182,26 @@
         for cp in q_copies:
             cp.start()
 
+    half = group // 2
+    hw = half * HEAD_DIM
+
+    def part(t, n):
+        return pl.ds(pl.multiple_of(t * gw + n * hw, HEAD_DIM), hw)
+
     g_copies = []
-    for i in range(1, tp_n):
-        t = tp_at(i)
-        cp = rcopy(g_in.at[:, cols(head_at(t), gw)], gh.at[my_rows, :], g_s.at[i - 1], g_r.at[i - 1], {"ctx": c, "tp": t})
-        cp.start()
-        g_copies.append(cp)
+    for n in range(2):
+        for i in range(1, tp_n):
+            t = tp_at(i)
+            cp = rcopy(g_in.at[:, part(head_at(t), n)], gh.at[my_rows, n * hw:(n + 1) * hw], g_s.at[n, i - 1],
+                       g_r.at[n, i - 1], {"ctx": c, "tp": t})
+            cp.start()
+            g_copies.append(cp)
 
     @pl.when(from_prev)
     def _():
         to_next.wait_recv()
-        for i in range(1, NX):
-            x_prev(i).start()
+        x_prev(1).start()
+        x_prev(NX - 1).start()
 
     @pl.when(from_second)
     def _():
@@ -198,6 +211,13 @@
             def _():
                 x_far(i).start()
 
+    @pl.when(from_prev)
+    def _():
+        x_prev(1).wait_recv()
+        pass_k.start()
+        x_prev(NX - 1).wait_recv()
+        pass_v.start()
+
     for i in range(1, NX):
         @pl.when((lax.rem(x + NX - i, NX) < x) | (row >= 2))
         def _():
@@ -205,8 +225,8 @@
 
     @pl.when(from_prev)
     def _():
-        for i in range(1, NX):
-            x_prev(i).wait_recv()
+        pass_k.wait_recv()
+        pass_v.wait_recv()
 
     for slot in range(2 * NX):
         kt[:, slot * stretch:(slot + 1) * stretch] = jnp.transpose(kvs[slot, 0].astype(F32)).astype(BF16)
@@ -231,20 +251,20 @@
         attn_b[:, at] = jnp.transpose(out_t / total).astype(BF16)
         return carry
 
-    lax.fori_loop(0, group, forward, 0)
-
     a_copies = []
-    for i in range(1, tp_n):
-        t = tp_at(i)
-        cp = rcopy(attn_b.at[cols(t, tok), :], attn_out.at[:, cols(me, gw)], oa_s.at[i - 1], oa_r.at[i - 1],
-                   {"ctx": c, "tp": t})
-        cp.start()
-        a_copies.append(cp)
+    for n in range(2):
+        lax.fori_loop(n * half, (n + 1) * half, forward, 0)
+        for i in range(1, tp_n):
+            t = tp_at(i)
+            cp = rcopy(attn_b.at[cols(t, tok), n * hw:(n + 1) * hw], attn_out.at[:, part(me, n)], oa_s.at[n, i - 1],
+                       oa_r.at[n, i - 1], {"ctx": c, "tp": t})
+            cp.start()
+            a_copies.append(cp)
     keep_a = pltpu.make_async_copy(attn_b.at[my_rows, :], attn_out.at[:, cols(me, gw)], loc.at[0])
     keep_a.start()
 
     locals_[3].wait()
-    for cp in g_copies:
+    for cp in g_copies[:tp_n - 1]:
         cp.wait_recv()
 
     def dots(h, carry):
@@ -253,7 +273,7 @@
         odot[h] = jnp.sum(jnp.transpose(prod), axis=0, keepdims=True)
         return carry
 
-    lax.fori_loop(0, group, dots, 0)
+    lax.fori_loop(0, half, dots, 0)
 
     def d_m(i):
         return rcopy(dsend.at[mate_x(i)], r_m.at[i - 1], dm_s.at[i - 1], dm_r.at[i - 1],
@@ -262,9 +282,6 @@
     def d_b(i):
         return rcopy(dsend.at[NX + mate_x(i)], r_b.at[i - 1], db_s.at[i - 1], db_r.at[i - 1],
                      {"ctx": ctx_at(row, mate_x(i)), "tp": p})
-
-    half = group // 2
-    hw = half * HEAD_DIM
 
     def grads(h, slot, q, g, k_t):
         pr = wts[h, slot] * inv_t[h]
@@ -298,12 +315,15 @@
     for n in range(2):
         for i in range(1, tp_n):
             t = tp_at(i)
-            to = pl.ds(pl.multiple_of(me * gw + n * hw, HEAD_DIM), hw)
             dq_copies.append(rcopy(
-                dq_b.at[cols(t, tok), n * hw:(n + 1) * hw], dq_out.at[:, to], oq_s.at[n, i - 1], oq_r.at[n, i - 1],
+                dq_b.at[cols(t, tok), n * hw:(n + 1) * hw], dq_out.at[:, part(me, n)], oq_s.at[n, i - 1], oq_r.at[n, i - 1],
                 {"ctx": c, "tp": t}))
     for cp in dq_copies[:tp_n - 1]:
         cp.start()
+
+    for cp in g_copies[tp_n - 1:]:
+        cp.wait_recv()
+    lax.fori_loop(half, group, dots, 0)
 
     def backward(slot):
         k_t = kt[:, pl.ds(pl.multiple_of(slot * stretch, stretch), stretch)]
@@ -413,8 +433,10 @@
 
     @pl.when(from_prev)
     def _():
-        for i in range(1, NX):
-            x_prev(i).wait_send()
+        x_prev(1).wait_send()
+        x_prev(NX - 1).wait_send()
+        pass_k.wait_send()
+        pass_v.wait_send()
         back_one.wait_send()
 
     @pl.when(from_second)
@@ -452,11 +474,11 @@
             V((stretch, gw), BF16), V((group // 2, HEAD_DIM, stretch), F32), V((stretch, gw), BF16),
             V((n2,) + piece, F32), V(piece, F32), V((n2,) + piece, BF16), V((NX - 1,) + piece, BF16), V((NX - 1,) + piece, BF16),
             V(piece, BF16), V(piece, BF16), V(piece, BF16), V(piece, BF16), V(piece, BF16),
-            dma((2, tp_n - 1)), dma((2, tp_n - 1)), dma((tp_n - 1,)), dma((tp_n - 1,)), dma((tp_n - 1,)),
-            dma((tp_n - 1,)), dma((4,)),
+            dma((2, tp_n - 1)), dma((2, tp_n - 1)), dma((tp_n - 1,)), dma((tp_n - 1,)), dma((2, tp_n - 1)),
+            dma((2, tp_n - 1)), dma((4,)),
+            dma((NX - 1,)), dma((NX - 1,)), dma((NX,)), dma((NX,)), dma((2,)), dma((2,)),
             dma((NX - 1,)), dma((NX - 1,)), dma((NX - 1,)), dma((NX - 1,)), dma((2,)), dma((2,)),
-            dma((NX - 1,)), dma((NX - 1,)), dma((NX - 1,)), dma((NX - 1,)), dma((2,)), dma((2,)),
-            dma((tp_n - 1,)), dma((tp_n - 1,)), dma((2, tp_n - 1)), dma((2, tp_n - 1)), dma((tp_n - 1,)), dma((tp_n - 1,)),
+            dma((2, tp_n - 1)), dma((2, tp_n - 1)), dma((2, tp_n - 1)), dma((2, tp_n - 1)), dma((tp_n - 1,)), dma((tp_n - 1,)),
         ]
         attn, dq, dkv = pl.pallas_call(
             functools.partial(kernel, rows_n, tp_n, group, tok),

time: 86.8 us -> 85.4 us (0.984)
  Pallas kernels: 82.4 us -> 80.9 us
    pallas_call x1, Pallas kernels: 82.4 us -> 80.9 us  [local(): pl.pallas_call(functools.partial(kernel, rows_n, tp_n, group, tok), out_s...]
where the time goes in v3:
time: 85.4 us; the launch traced here: 85.2 us
  Pallas kernels  80.9 us (95%)
  other arithmetic  2.86 us (3%)
    pallas_call x1, Pallas kernels, local(): pl.pallas_call(functools.partial(kernel, rows_n, tp_n, group, tok), out_s...  80.9 us
    convert_element_type x2, other arithmetic, local(): return (attn, dq.astype(F32), dkv[0].astype(F32), dkv[1].astype(F32))  2.86 us

profile of v3, /device:TPU:31, one launch (start us, length us, event | category | flops | bytes accessed | tf_op | source)
XLA Modules:
  0.0 85.2 jit_solution(976526561300013586)
XLA Ops:
  0.6 80.9 %attention_layer.1 = (bf16[32,8192]{1,0:T(8,128)(2,1)}, bf16[32,8192]{1,0:T(8,128)(2,1)}, bf16[2,32,1024]{2,1,0:T(8,128)(2,1)}) custom-call(s32[64]{0:T(128)} %docs.1, bf16[32,8192]{1,0:T(8,128)(2,1)} %q_in.1, bf16[32,1024]{1,0:T(8,128)(2,1)} %k_in.1, bf16[32,1024]{1,0:T(8,128)(2,1)} %v_in.1, bf16[32,8192]{1,0:T(8,128)(2,1)} %g_in.1), custom_call_target="tpu_custom_call" | custom-call | tf_op jit(solution)/shard_map/attention_layer/pallas_call | solution.py:483
  81.6 0.0 copy-start.1
  81.6 0.0 copy-start
  81.6 2.1 %convert_element_type.15 = f32[32,8192]{1,0:T(8,128)} convert(bf16[32,8192]{1,0:T(8,128)(2,1)} %get-tuple-element.8) | non-fusion elementwise | flops 262144 | bytes 1572864 | tf_op jit(solution)/shard_map/convert_element_type | solution.py:497
  83.7 0.0 copy-done.1
  83.7 0.7 bitcast_convert_fusion
  84.4 0.0 copy-done
  84.4 0.8 copy.10
Async XLA Ops:
  81.6 2.2 %copy-start.1 = (bf16[2,32,1024]{2,1,0:T(8,128)(2,1)S(1)}, bf16[2,32,1024]{2,1,0:T(8,128)(2,1)}, u32[]{:S(2)}) copy-start(bf16[2,32,1024]{2,1,0:T(8,128)(2,1)} %get-tuple-element.9) | copy-start | bytes 393220
  81.6 2.9 %copy-start = (bf16[32,8192]{1,0:T(8,128)(2,1)S(1)}, bf16[32,8192]{1,0:T(8,128)(2,1)}, u32[]{:S(2)}) copy-start(bf16[32,8192]{1,0:T(8,128)(2,1)} %get-tuple-element.16) | copy-start | bytes 1572868
